TPU v7x, 512 devices: a whole 4x4x16 slice. The times are simulated.
512 devices in a mesh: dp: 16 (over x, y), tm: 32 (over z, core).
Axes of the slice: x: 4, y: 4, z: 16, core: 2. Of those that a mesh axis runs over, the one named last changes fastest.
Arguments:
- records: bfloat16 [16, 4096, 1024], P('dp', 'tm'), may hold values from -6 to 6
- x_weight: bfloat16 [1024, 512], replicated, may hold values from -0.1875 to 0.1875
- bc_weight: bfloat16 [1024, 256], replicated, may hold values from -0.1875 to 0.1875
- decay_codes: int32 [16, 4096, 8], P('dp', 'tm'), may hold values from 0 to 524
- out_grad: bfloat16 [16, 4096, 512], P('dp', 'tm'), may hold values from -6 to 6
Outputs:
- y_out: bfloat16 [16, 4096, 512], P('dp', 'tm')
- x_grad: float32 [1024, 512], P('tm')
- bc_grad: float32 [1024, 256], P('tm')
All inputs are finite; a program needn't handle non-finite values.
Results may differ from a plain program's by a relative error of at most 0.0085.
Values sent between devices are 32-bit elements; how exact they have to be, the bound alone decides.
No kernel may reach another device: no remote copies, remote signals or barrier semaphores. Data moves between devices by JAX's collectives and lax.ppermute only.
A program may use at most 64 MiB of HBM per device.

v0:
```python
import jax
import jax.numpy as jnp
from jax import lax
from jax.sharding import PartitionSpec as P

SPAN = 128
highest = lax.Precision.HIGHEST


def entering(part, axis, combine, identity, reverse):
    count = lax.axis_size(axis)
    place = lax.axis_index(axis)
    ahead = count - 1 - place if reverse else place
    gathered = jax.tree.map(lambda a: lax.all_gather(a, axis), part)
    state = jax.tree.map(lambda a, e: jnp.zeros_like(a) + jnp.asarray(e, a.dtype), part, identity)

    def one(turn, state):
        source = count - 1 - turn if reverse else turn
        return combine(
            state, jax.tree.map(lambda a: lax.dynamic_index_in_dim(a, source, 0, False), gathered)
        )

    return lax.fori_loop(0, ahead, one, state)


def span_kernel(log_decay):
    running = jnp.cumsum(log_decay, axis=1)
    length = log_decay.shape[1]
    causal = lax.broadcasted_iota(jnp.int32, (length, length), 0) >= lax.broadcasted_iota(
        jnp.int32, (length, length), 1
    )
    causal = causal[None, None, :, :]
    heads_first = jnp.transpose(running, (0, 2, 1))
    gaps = heads_first[:, :, :, None] - heads_first[:, :, None, :]
    kernel = jnp.where(causal, jnp.exp(jnp.where(causal, gaps, 0.0)), 0.0)
    return (running, kernel)


def block_scores(readout, inject):
    return jnp.einsum(
        "rtn,rsn->rts",
        readout.astype(jnp.bfloat16),
        inject.astype(jnp.bfloat16),
        preferred_element_type=jnp.float32,
    )


def forward_span(carry_state, pieces):
    mixer_f, inject, readout, cot_heads, log_decay = pieces
    running, kernel = span_kernel(log_decay)
    scores = block_scores(readout, inject)
    mixing = kernel * scores[:, None, :, :]
    decayed = jnp.exp(running)
    within = jnp.einsum("rhts,rshp->rthp", mixing, mixer_f, precision=highest)
    carried = decayed[..., None] * jnp.einsum(
        "rhpn,rtn->rthp", carry_state, readout, precision=highest
    )
    pair_dots = jnp.einsum("rthp,rshp->rhts", cot_heads, mixer_f, precision=highest)
    grad_read = jnp.einsum("rhts,rsn->rtn", kernel * pair_dots, inject, precision=highest)
    grad_read = grad_read + jnp.einsum(
        "rthp,rhpn->rtn", decayed[..., None] * cot_heads, carry_state, precision=highest
    )
    to_end = jnp.exp(running[:, -1:, :] - running)
    new_state = jnp.exp(running[:, -1, :])[:, :, None, None] * carry_state
    new_state = new_state + jnp.einsum(
        "rshp,rsn->rhpn", to_end[..., None] * mixer_f, inject, precision=highest
    )
    return (new_state, (within + carried, grad_read))


def reverse_span(adjoint, pieces):
    mixer_f, inject, readout, cot_heads, log_decay = pieces
    running, kernel = span_kernel(log_decay)
    scores = block_scores(readout, inject)
    mixing = kernel * scores[:, None, :, :]
    pair_dots = jnp.einsum("rthp,rshp->rhts", cot_heads, mixer_f, precision=highest)
    to_end = jnp.exp(running[:, -1:, :] - running)
    grad_mixer = jnp.einsum("rhts,rthp->rshp", mixing, cot_heads, precision=highest)
    grad_mixer = grad_mixer + to_end[..., None] * jnp.einsum(
        "rhpn,rsn->rshp", adjoint, inject, precision=highest
    )
    grad_inject = jnp.einsum("rhts,rtn->rsn", kernel * pair_dots, readout, precision=highest)
    grad_inject = grad_inject + jnp.einsum(
        "rshp,rhpn->rsn", to_end[..., None] * mixer_f, adjoint, precision=highest
    )
    new_adjoint = jnp.exp(running[:, -1, :])[:, :, None, None] * adjoint
    new_adjoint = new_adjoint + jnp.einsum(
        "rthp,rtn->rhpn", jnp.exp(running)[..., None] * cot_heads, readout, precision=highest
    )
    return (new_adjoint, (grad_mixer, grad_inject))


def to_blocks(array, frames):
    return array.reshape((frames // SPAN, 1, SPAN) + array.shape[1:])


def combine_pair(earlier, later_one):
    return (earlier[0] * later_one[0], later_one[0][:, :, None, None] * earlier[1] + later_one[1])


def body(records, x_weight, bc_weight, decay_codes, out_grad):
    signal = records[0]
    codes = decay_codes[0]
    frames_dev, model_dim = signal.shape
    head_count = codes.shape[1]
    mixer_dim = x_weight.shape[1]
    head_size = mixer_dim // head_count
    state_size = bc_weight.shape[1] // 2
    tm_count = lax.axis_size("tm")
    groups = lax.axis_size("dp")
    out_scale = (state_size * frames_dev * tm_count) ** (-0.5)
    grad_scale = (groups * frames_dev * tm_count) ** (-0.5)
    decay_unit = 1.0 / (32.0 * frames_dev * tm_count)
    mixer_in = jnp.dot(signal, x_weight, preferred_element_type=jnp.float32).astype(jnp.bfloat16)
    state_proj = jnp.dot(signal, bc_weight, preferred_element_type=jnp.float32).astype(jnp.bfloat16)
    log_decay = -decay_unit * codes.astype(jnp.float32)
    cotangent = out_grad[0].astype(jnp.float32) * out_scale
    mixer_f = mixer_in.astype(jnp.float32).reshape(frames_dev, head_count, head_size)
    inject = state_proj[:, :state_size].astype(jnp.float32)
    readout = state_proj[:, state_size:].astype(jnp.float32)
    cot_heads = cotangent.reshape(frames_dev, head_count, head_size)
    blocks = (
        to_blocks(mixer_f, frames_dev),
        to_blocks(inject, frames_dev),
        to_blocks(readout, frames_dev),
        to_blocks(cot_heads, frames_dev),
        to_blocks(log_decay, frames_dev),
    )
    zero_state = jnp.zeros((1, head_count, head_size, state_size), jnp.float32)
    end_state, (local_out, local_read) = lax.scan(forward_span, zero_state, blocks)
    start_adjoint, (local_grad, local_inject) = lax.scan(
        reverse_span, zero_state, blocks, reverse=True
    )
    running = jnp.cumsum(log_decay, axis=0)
    device_log = running[-1]
    identity = (jnp.ones((1, head_count), jnp.float32), zero_state)
    carry_in = entering(
        (jnp.exp(device_log)[None], end_state), "tm", combine_pair, identity, False
    )[1][0]
    adjoint_in = entering(
        (jnp.exp(device_log)[None], start_adjoint), "tm", combine_pair, identity, True
    )[1][0]
    decayed = jnp.exp(running)
    to_end = jnp.exp(device_log[None] - running)
    output = local_out.reshape(frames_dev, head_count, head_size)
    output = output + decayed[..., None] * jnp.einsum(
        "hpn,tn->thp", carry_in, readout, precision=highest
    )
    grad_read = local_read.reshape(frames_dev, state_size)
    grad_read = grad_read + jnp.einsum(
        "thp,hpn->tn", decayed[..., None] * cot_heads, carry_in, precision=highest
    )
    grad_mixer = local_grad.reshape(frames_dev, head_count, head_size)
    grad_mixer = grad_mixer + to_end[..., None] * jnp.einsum(
        "hpn,tn->thp", adjoint_in, inject, precision=highest
    )
    grad_inject = local_inject.reshape(frames_dev, state_size)
    grad_inject = grad_inject + jnp.einsum(
        "thp,hpn->tn", to_end[..., None] * mixer_f, adjoint_in, precision=highest
    )
    grad_mix = grad_mixer.reshape(frames_dev, mixer_dim).astype(jnp.bfloat16)
    grad_proj = jnp.concatenate([grad_inject, grad_read], axis=1).astype(jnp.bfloat16)
    grad_cat = jnp.concatenate([grad_mix, grad_proj], axis=1)
    grad_share = lax.psum_scatter(
        lax.dot_general(
            signal, grad_cat, (((0,), (0,)), ((), ())), preferred_element_type=jnp.float32
        ),
        "tm",
        scatter_dimension=0,
        tiled=True,
    )
    grad_share = lax.psum(grad_share, "dp")
    grad_share = grad_share * grad_scale
    y_out = output.reshape(frames_dev, mixer_dim).astype(jnp.bfloat16)[None]
    return (y_out, grad_share[:, :mixer_dim], grad_share[:, mixer_dim:])


def solution(mesh):
    return jax.shard_map(
        body,
        mesh=mesh,
        in_specs=(P("dp", "tm", None), P(), P(), P("dp", "tm", None), P("dp", "tm", None)),
        out_specs=(P("dp", "tm", None), P("tm", None), P("tm", None)),
        check_vma=False,
    )
```

profile of v0, /device:TPU:32, one launch (start us, length us, event | category | flops | bytes accessed | tf_op | source)
XLA Modules:
  0.0 444.9 jit_solution(17753559127679987640)
XLA Ops:
  7.2 0.8 fusion.69
  9.1 1.4 convolution_convert_fusion.1
  10.5 1.3 convert_multiply_fusion
  11.9 1.0 convolution_add_fusion.1
  13.0 1.0 copy.79
  14.1 1.0 convolution_add_fusion
  15.5 33.9 %all-gather.3 = f32[32,1,8]{2,1,0:T(1,128)S(1)} all-gather(f32[1,1,8]{2,1,0:T(1,128)S(1)} %get-tuple-element.267), channel_id=2, replica_groups=mesh['dp'=16,'tm'=32] {'tm'}, dimensions={0}, use_global_device_ids=true | all-gather | bytes 1056 | tf_op jit(solution)/shard_map/all_gather | solution.py:14
  49.5 0.3 fusion.2
  49.8 0.4 convolution_bitcast_fusion.4
  50.2 0.4 convolution_bitcast_fusion.6
  50.6 0.7 fusion
  51.4 0.8 fusion.4
  52.1 44.4 %all-gather.7.cloned.1.call-done = f32[256,64,128]{2,1,0:T(8,128)} async-done(((f32[8,64,128]{2,1,0:T(8,128)}), f32[256,64,128]{2,1,0:T(8,128)}) %all-gather.7.cloned.1.call-update) | async-done | bytes 8388624 | tf_op jit(solution)/shard_map/all_gather | solution.py:14
  96.6 2.2 while.16
  96.6 1.1 bitcast_add_fusion.4
  97.7 1.1 bitcast_add_fusion.4
  98.8 76.1 %all-gather.9.cloned.1.call-done = f32[256,64,128]{2,1,0:T(8,128)} async-done(((f32[8,64,128]{2,1,0:T(8,128)}), f32[256,64,128]{2,1,0:T(8,128)}) %all-gather.9.cloned.1.call-update) | async-done | bytes 8388624 | tf_op jit(solution)/shard_map/all_gather | solution.py:14
  174.9 31.9 %while.17 = (s32[]{:T(128)}, f32[1,8,64,128]{3,2,1,0:T(8,128)S(1)}, s32[]{:T(128)}, f32[32,1,8]{2,1,0:T(1,128)S(1)}, f32[32,1,8,64,128]{4,3,2,1,0:T(8,128)}, /*index=5*/s32[]{:T(128)}, s32[]{:T(128)}, s32[]{:T(128)}, s32[]{:T(128)}) while((s32[]{:T(128)}, f32[1,8,64,128]{3,2,1,0:T(8,128)S(1)}, s32[]{:T(128)}, f32[32,1,8]{2,1,0:T(1,128)S(1)}, ...), condition=%wide.region_5.6_spmd, body=%wide.region_4.5_spmd.sunk | while | flops 131078 | bytes 786683 | solution.py:23
  174.9 1.1 bitcast_add_fusion.5
  176.0 1.1 bitcast_add_fusion.5
  177.1 1.1 bitcast_add_fusion.5
  178.2 1.1 bitcast_add_fusion.5
  179.3 1.1 bitcast_add_fusion.5
  180.4 1.1 bitcast_add_fusion.5
  181.5 1.1 bitcast_add_fusion.5
  182.6 1.1 bitcast_add_fusion.5
  183.7 1.1 bitcast_add_fusion.5
  184.8 1.1 bitcast_add_fusion.5
  185.9 1.1 bitcast_add_fusion.5
  187.0 1.1 bitcast_add_fusion.5
  188.1 1.1 bitcast_add_fusion.5
  189.2 1.1 bitcast_add_fusion.5
  190.4 1.1 bitcast_add_fusion.5
  191.5 1.1 bitcast_add_fusion.5
  192.6 1.1 bitcast_add_fusion.5
  193.7 1.1 bitcast_add_fusion.5
  194.8 1.1 bitcast_add_fusion.5
  195.9 1.1 bitcast_add_fusion.5
  197.0 1.1 bitcast_add_fusion.5
  198.1 1.1 bitcast_add_fusion.5
  199.2 1.1 bitcast_add_fusion.5
  200.3 1.1 bitcast_add_fusion.5
  201.4 1.1 bitcast_add_fusion.5
  202.5 1.1 bitcast_add_fusion.5
  203.6 1.1 bitcast_add_fusion.5
  204.7 1.1 bitcast_add_fusion.5
  205.8 1.1 bitcast_add_fusion.5
  206.8 0.6 convolution_bitcast_fusion.5
  207.4 0.3 fusion.10
  207.7 0.6 convolution_bitcast_fusion.3
  208.3 0.2 fusion.14
  208.6 0.2 fusion.13
  208.8 2.2 convolution_bitcast_fusion
  211.1 3.5 copy.87
  214.7 0.3 fusion.6
  214.9 0.7 fusion.8
  215.7 101.2 %reduce-scatter.4.cloned.1.call-done = f32[32,768]{1,0:T(8,128)} async-done(((f32[1024,768]{1,0:T(8,128)}), f32[32,768]{1,0:T(8,128)}) %reduce-scatter.4.cloned.1.call-update) | async-done | bytes 98320
  316.9 1.8 copy.88
  318.7 0.3 fusion.9
  319.0 0.8 copy.84
  319.7 116.2 %all-reduce.2.cloned.1.call-done = f32[32,768]{0,1:T(8,128)} async-done(((f32[32,768]{0,1:T(8,128)}), f32[32,768]{0,1:T(8,128)}) %all-reduce.2.cloned.1.call-update) | async-done | bytes 98320 | tf_op jit(solution)/shard_map/psum | solution.py:172
  435.9 1.0 broadcast_multiply_fusion
  437.0 0.7 copy.85
  437.7 0.7 copy.86
  (70 shorter events, 2.3 us)
Async XLA Ops:
  7.2 3.3 copy-start
  7.2 89.4 %all-gather.7.cloned.1.call-start = ((), (), s32[]{:S(2)}) async-start(), calls=%async_computation.2 | async-start | bytes 8650752 | tf_op jit(solution)/shard_map/all_gather | solution.py:14
  12.9 161.9 %all-gather.9.cloned.1.call-start = ((), (), s32[]{:S(2)}) async-start(), calls=%async_computation.3 | async-start | bytes 8650752 | tf_op jit(solution)/shard_map/all_gather | solution.py:14
  14.1 194.7 %copy-start.1 = (bf16[1,128,1024]{2,1,0:T(8,128)(2,1)S(1)}, bf16[1,128,1024]{2,1,0:T(8,128)(2,1)}, u32[]{:S(2)}) copy-start(bf16[1,128,1024]{2,1,0:T(8,128)(2,1)} %param.9) | copy-start | bytes 786436
  15.1 301.7 %reduce-scatter.4.cloned.1.call-start = ((), (), s32[]{:S(2)}) async-start(), calls=%async_computation.4 | async-start | bytes 3244032
  214.6 221.3 %all-reduce.2.cloned.1.call-start = ((), (), s32[]{:S(2)}) async-start(), calls=%async_computation.1 | async-start | bytes 786432 | tf_op jit(solution)/shard_map/psum | solution.py:172
Sparse Core Ops, SparseCore 0:
  13.0 83.4 all-gather.6
  98.7 76.1 all-gather.8
  214.7 102.0 reduce-scatter.3
  320.3 115.5 all-reduce.1
where the time goes:
time: 446 us; the launch traced here: 445 us
  waiting for transfers between devices  338 us (76%)
  other arithmetic  35.2 us (8%)
  blocking collectives  33.9 us (8%)
  between operations  14 us (3%)
  matrix products  12.6 us (3%)
  local copies, waits for them, and re-layouts  10 us (2%)
    all_gather x2, waiting for transfers between devices, entering(): gathered = jax.tree.map(lambda a: lax.all_gather(a, axis), part)  121 us
    psum x1, waiting for transfers between devices, body(): grad_share = lax.psum(grad_share, 'dp')  116 us
    unnamed x5, waiting for transfers between devices  101 us
    all_gather x1, blocking collectives, entering(): gathered = jax.tree.map(lambda a: lax.all_gather(a, axis), part)  33.9 us
    add x31, other arithmetic, combine_pair(): later_one[0][:, :, None, None] * earlier[1] + later_one[1]  32.9 us
  transfers between devices with their start and end apart: 4, of which 4 were waited for; matrix products, arithmetic and copies ran while one was open for 2% of the time, Pallas kernels for 0%

commit v1 on v0

--- a/solution.py
+++ b/solution.py
@@ -169,7 +169,11 @@
         scatter_dimension=0,
         tiled=True,
     )
-    grad_share = lax.psum(grad_share, "dp")
+    grad_share = grad_share
+    for hop in (1, 2, 4, 8):
+        grad_share = grad_share + lax.ppermute(
+            grad_share, "dp", [(dev, dev ^ hop) for dev in range(16)]
+        )
     grad_share = grad_share * grad_scale
     y_out = output.reshape(frames_dev, mixer_dim).astype(jnp.bfloat16)[None]
     return (y_out, grad_share[:, :mixer_dim], grad_share[:, mixer_dim:])

time: 446 us -> 379 us (0.85)
  the two profiles are of different devices: /device:TPU:32 before, /device:TPU:96 now
where the time goes in v1:
time: 379 us; the launch traced here: 378 us
  waiting for transfers between devices  261 us (69%)
  other arithmetic  34.4 us (9%)
  blocking collectives  30.9 us (8%)
  starting transfers between devices  14.6 us (4%)
  between operations  14.1 us (4%)
  matrix products  12.7 us (3%)
  local copies, waits for them, and re-layouts  9.25 us (2%)
    all_gather x2, waiting for transfers between devices, entering(): gathered = jax.tree.map(lambda a: lax.all_gather(a, axis), part)  117 us
    unnamed x4, waiting for transfers between devices  107 us
    ppermute x4, waiting for transfers between devices, body(): lax.ppermute(grad_share, 'dp', [(dev, dev ^ hop) for dev in range(16)])  37 us
    add x31, other arithmetic, combine_pair(): later_one[0][:, :, None, None] * earlier[1] + later_one[1]  32.9 us
    all_gather x1, blocking collectives, entering(): gathered = jax.tree.map(lambda a: lax.all_gather(a, axis), part)  30.9 us
    ppermute x4, starting transfers between devices, body(): lax.ppermute(grad_share, 'dp', [(dev, dev ^ hop) for dev in range(16)])  14.4 us
    unnamed x10, local copies, waits for them, and re-layouts  7.82 us
  transfers between devices with their start and end apart: 7, of which 7 were waited for; matrix products, arithmetic and copies ran while one was open for 4% of the time, Pallas kernels for 0%

profile of v1, /device:TPU:96, one launch (start us, length us, event | category | flops | bytes accessed | tf_op | source)
XLA Modules:
  0.0 377.7 jit_solution(9484812434733328361)
XLA Ops:
  7.2 0.8 fusion.69
  9.1 1.4 convolution_convert_fusion.1
  10.5 1.3 convert_multiply_fusion
  11.9 1.0 convolution_add_fusion.1
  13.0 1.0 copy.79
  14.1 1.0 convolution_add_fusion
  15.5 30.9 %all-gather.3 = f32[32,1,8]{2,1,0:T(1,128)S(1)} all-gather(f32[1,1,8]{2,1,0:T(1,128)S(1)} %get-tuple-element.267), channel_id=2, replica_groups=mesh['dp'=16,'tm'=32] {'tm'}, dimensions={0}, use_global_device_ids=true | all-gather | bytes 1056 | tf_op jit(solution)/shard_map/all_gather | solution.py:14
  46.7 0.4 convolution_bitcast_fusion.4
  47.1 0.4 convolution_bitcast_fusion.6
  47.5 0.7 fusion
  48.3 0.8 fusion.4
  49.1 45.6 %all-gather.7.cloned.1.call-done = f32[256,64,128]{2,1,0:T(8,128)} async-done(((f32[8,64,128]{2,1,0:T(8,128)}), f32[256,64,128]{2,1,0:T(8,128)}) %all-gather.7.cloned.1.call-update) | async-done | bytes 8388624 | tf_op jit(solution)/shard_map/all_gather | solution.py:14
  94.8 6.6 %while.16 = (s32[]{:T(128)}, f32[1,8,64,128]{3,2,1,0:T(8,128)S(1)}, s32[]{:T(128)}, f32[32,1,8]{2,1,0:T(1,128)S(1)}, f32[32,1,8,64,128]{4,3,2,1,0:T(8,128)}, /*index=5*/s32[]{:T(128)}, s32[]{:T(128)}, s32[]{:T(128)}) while((s32[]{:T(128)}, f32[1,8,64,128]{3,2,1,0:T(8,128)S(1)}, s32[]{:T(128)}, f32[32,1,8]{2,1,0:T(1,128)S(1)}, ...), condition=%wide.region_3.4_spmd, body=%wide.region_2.3_spmd.sunk | while | flops 131077 | bytes 786663 | solution.py:23
  94.8 1.1 bitcast_add_fusion.4
  95.9 1.1 bitcast_add_fusion.4
  97.0 1.1 bitcast_add_fusion.4
  98.1 1.1 bitcast_add_fusion.4
  99.2 1.1 bitcast_add_fusion.4
  100.3 1.1 bitcast_add_fusion.4
  101.4 71.6 %all-gather.9.cloned.1.call-done = f32[256,64,128]{2,1,0:T(8,128)} async-done(((f32[8,64,128]{2,1,0:T(8,128)}), f32[256,64,128]{2,1,0:T(8,128)}) %all-gather.9.cloned.1.call-update) | async-done | bytes 8388624 | tf_op jit(solution)/shard_map/all_gather | solution.py:14
  173.0 27.5 %while.17 = (s32[]{:T(128)}, f32[1,8,64,128]{3,2,1,0:T(8,128)S(1)}, s32[]{:T(128)}, f32[32,1,8]{2,1,0:T(1,128)S(1)}, f32[32,1,8,64,128]{4,3,2,1,0:T(8,128)}, /*index=5*/s32[]{:T(128)}, s32[]{:T(128)}, s32[]{:T(128)}, s32[]{:T(128)}) while((s32[]{:T(128)}, f32[1,8,64,128]{3,2,1,0:T(8,128)S(1)}, s32[]{:T(128)}, f32[32,1,8]{2,1,0:T(1,128)S(1)}, ...), condition=%wide.region_5.6_spmd, body=%wide.region_4.5_spmd.sunk | while | flops 131078 | bytes 786683 | solution.py:23
  173.1 1.1 bitcast_add_fusion.5
  174.2 1.1 bitcast_add_fusion.5
  175.3 1.1 bitcast_add_fusion.5
  176.4 1.1 bitcast_add_fusion.5
  177.5 1.1 bitcast_add_fusion.5
  178.6 1.1 bitcast_add_fusion.5
  179.7 1.1 bitcast_add_fusion.5
  180.8 1.1 bitcast_add_fusion.5
  181.9 1.1 bitcast_add_fusion.5
  183.0 1.1 bitcast_add_fusion.5
  184.1 1.1 bitcast_add_fusion.5
  185.2 1.1 bitcast_add_fusion.5
  186.3 1.1 bitcast_add_fusion.5
  187.4 1.1 bitcast_add_fusion.5
  188.5 1.1 bitcast_add_fusion.5
  189.6 1.1 bitcast_add_fusion.5
  190.7 1.1 bitcast_add_fusion.5
  191.8 1.1 bitcast_add_fusion.5
  192.9 1.1 bitcast_add_fusion.5
  194.0 1.1 bitcast_add_fusion.5
  195.1 1.1 bitcast_add_fusion.5
  196.2 1.1 bitcast_add_fusion.5
  197.3 1.1 bitcast_add_fusion.5
  198.4 1.1 bitcast_add_fusion.5
  199.5 1.1 bitcast_add_fusion.5
  200.6 0.6 convolution_bitcast_fusion.5
  201.5 0.6 convolution_bitcast_fusion.3
  202.6 2.2 convolution_bitcast_fusion
  204.8 3.5 copy.87
  208.3 106.5 %reduce-scatter.4.cloned.1.call-done = f32[32,768]{1,0:T(8,128)} async-done(((f32[1024,768]{1,0:T(8,128)}), f32[32,768]{1,0:T(8,128)}) %reduce-scatter.4.cloned.1.call-update) | async-done | bytes 98320
  314.9 1.1 copy.88
  315.9 3.0 collective-permute-start
  318.9 8.4 %collective-permute-done = f32[32,768]{0,1:T(8,128)S(1)} collective-permute-done((f32[32,768]{0,1:T(8,128)S(1)}, f32[32,768]{0,1:T(8,128)S(1)}, u32[]{:S(2)}, u32[]{:S(2)}) %collective-permute-start) | collective-permute-done | bytes 98336 | tf_op jit(solution)/shard_map/ppermute | solution.py:174
  327.4 4.5 %collective-permute-start.1 = (f32[32,768]{0,1:T(8,128)S(1)}, f32[32,768]{0,1:T(8,128)S(1)}, u32[]{:S(2)}, u32[]{:S(2)}) collective-permute-start(f32[32,768]{0,1:T(8,128)S(1)} %add.107), channel_id=1, source_target_pairs={{0,64},{32,96},{64,0},{96,32},{128,192},{160,224},{192,128},{224,1... | collective-permute-start | bytes 294920 | tf_op jit(solution)/shard_map/ppermute | solution.py:174
  332.1 9.2 %collective-permute-done.1 = f32[32,768]{0,1:T(8,128)S(1)} collective-permute-done((f32[32,768]{0,1:T(8,128)S(1)}, f32[32,768]{0,1:T(8,128)S(1)}, u32[]{:S(2)}, u32[]{:S(2)}) %collective-permute-start.1) | collective-permute-done | bytes 98336 | tf_op jit(solution)/shard_map/ppermute | solution.py:174
  341.4 2.5 collective-permute-start.2
  344.0 0.7 fusion.8
  344.7 10.4 %collective-permute-done.2 = f32[32,768]{0,1:T(8,128)S(1)} collective-permute-done((f32[32,768]{0,1:T(8,128)S(1)}, f32[32,768]{0,1:T(8,128)S(1)}, u32[]{:S(2)}, u32[]{:S(2)}) %collective-permute-start.2) | collective-permute-done | bytes 98336 | tf_op jit(solution)/shard_map/ppermute | solution.py:174
  355.1 4.5 %collective-permute-start.3 = (f32[32,768]{0,1:T(8,128)S(1)}, f32[32,768]{0,1:T(8,128)S(1)}, u32[]{:S(2)}, u32[]{:S(2)}) collective-permute-start(f32[32,768]{0,1:T(8,128)S(1)} %add.109), channel_id=1, source_target_pairs={{0,256},{32,288},{64,320},{96,352},{128,384},{160,416},{192,448},{... | collective-permute-start | bytes 294920 | tf_op jit(solution)/shard_map/ppermute | solution.py:174
  359.9 0.8 copy.84
  360.7 9.0 %collective-permute-done.3 = f32[32,768]{0,1:T(8,128)S(1)} collective-permute-done((f32[32,768]{0,1:T(8,128)S(1)}, f32[32,768]{0,1:T(8,128)S(1)}, u32[]{:S(2)}, u32[]{:S(2)}) %collective-permute-start.3) | collective-permute-done | bytes 98336 | tf_op jit(solution)/shard_map/ppermute | solution.py:174
  369.8 0.7 copy.85
  370.5 0.7 copy.86
  (78 shorter events, 4.1 us)
Async XLA Ops:
  7.2 3.3 copy-start
  7.2 87.6 %all-gather.7.cloned.1.call-start = ((), (), s32[]{:S(2)}) async-start(), calls=%async_computation.1 | async-start | bytes 8650752 | tf_op jit(solution)/shard_map/all_gather | solution.py:14
  12.9 160.1 %all-gather.9.cloned.1.call-start = ((), (), s32[]{:S(2)}) async-start(), calls=%async_computation.2 | async-start | bytes 8650752 | tf_op jit(solution)/shard_map/all_gather | solution.py:14
  14.1 188.5 %copy-start.1 = (bf16[1,128,1024]{2,1,0:T(8,128)(2,1)S(1)}, bf16[1,128,1024]{2,1,0:T(8,128)(2,1)}, u32[]{:S(2)}) copy-start(bf16[1,128,1024]{2,1,0:T(8,128)(2,1)} %param.9) | copy-start | bytes 786436
  15.1 299.7 %reduce-scatter.4.cloned.1.call-start = ((), (), s32[]{:S(2)}) async-start(), calls=%async_computation.3 | async-start | bytes 3244032
  315.9 11.4 %collective-permute-start = (f32[32,768]{0,1:T(8,128)S(1)}, f32[32,768]{0,1:T(8,128)S(1)}, u32[]{:S(2)}, u32[]{:S(2)}) collective-permute-start(f32[32,768]{0,1:T(8,128)S(1)} %copy.88), channel_id=1, source_target_pairs={{0,32},{32,0},{64,96},{96,64},{128,160},{160,128},{192,224},{224,1... | collective-permute-start | bytes 294920 | tf_op jit(solution)/shard_map/ppermute | solution.py:174
  327.4 14.0 %collective-permute-start.1 = (f32[32,768]{0,1:T(8,128)S(1)}, f32[32,768]{0,1:T(8,128)S(1)}, u32[]{:S(2)}, u32[]{:S(2)}) collective-permute-start(f32[32,768]{0,1:T(8,128)S(1)} %add.107), channel_id=1, source_target_pairs={{0,64},{32,96},{64,0},{96,32},{128,192},{160,224},{192,128},{224,1... | collective-permute-start | bytes 294920 | tf_op jit(solution)/shard_map/ppermute | solution.py:174
  341.4 13.6 %collective-permute-start.2 = (f32[32,768]{0,1:T(8,128)S(1)}, f32[32,768]{0,1:T(8,128)S(1)}, u32[]{:S(2)}, u32[]{:S(2)}) collective-permute-start(f32[32,768]{0,1:T(8,128)S(1)} %add.108), channel_id=1, source_target_pairs={{0,128},{32,160},{64,192},{96,224},{128,0},{160,32},{192,64},{224,... | collective-permute-start | bytes 294920 | tf_op jit(solution)/shard_map/ppermute | solution.py:174
  355.1 14.5 %collective-permute-start.3 = (f32[32,768]{0,1:T(8,128)S(1)}, f32[32,768]{0,1:T(8,128)S(1)}, u32[]{:S(2)}, u32[]{:S(2)}) collective-permute-start(f32[32,768]{0,1:T(8,128)S(1)} %add.109), channel_id=1, source_target_pairs={{0,256},{32,288},{64,320},{96,352},{128,384},{160,416},{192,448},{... | collective-permute-start | bytes 294920 | tf_op jit(solution)/shard_map/ppermute | solution.py:174
Sparse Core Ops, SparseCore 0:
  13.0 81.6 all-gather.6
  96.9 76.1 all-gather.8
  208.5 106.3 reduce-scatter.3
